TPU v7x, 32 devices: a whole 2x2x4 slice. The times are simulated.
32 devices in a mesh: groups: 2 (over y), seq: 4 (over z), batch: 2 (over x), sub: 2 (over core).
Axes of the slice: x: 2, y: 2, z: 4, core: 2. Of those that a mesh axis runs over, the one named last changes fastest.
Arguments:
- gen_hidden: bfloat16 [4, 256, 8192], P(('groups', 'batch'), None, ('seq', 'sub')), parts along dimension 0, may hold values from -6 to 6
- out_proj: bfloat16 [8192, 4096], P(('seq', 'sub')), may hold values from -0.0625 to 0.0625
- norm_gain: bfloat16 [4096], replicated, may hold values from 0.099609375 to 1.8984375
- q_weight: bfloat16 [4096, 4096], P(None, ('seq', 'sub')), may hold values from -0.09375 to 0.09375
- kv_weight: bfloat16 [2, 4096, 1024], P(None, None, ('seq', 'sub')), may hold values from -0.09375 to 0.09375
- kv_cache: bfloat16 [2, 4, 8192, 1024], P(None, ('groups', 'batch'), ('seq', 'sub')), parts along dimension 1, may hold values from -96 to 96
- lengths: int32 [4], P(('groups', 'batch')), parts along dimension 0, may hold values from 1024 to 8192, as said below
- span_start: int32 [4], P(('groups', 'batch')), parts along dimension 0, may hold values from 1024 to 16383, as said below
Outputs:
- attention: bfloat16 [4, 256, 4096], P(('groups', 'batch'), ('seq', 'sub')), parts along dimension 0
There are 2 independent parts, one for each index of `groups`. A program takes and returns all parts, laid end to end along the dimension named above; an argument that names none is the same for every part. Nothing has to cross between parts.
Inputs may be any that keep to these rules, and one draw needn't show every extreme that they name: `lengths`: slots at or past a session's length are not attended. In every draw some session has the full 8192 slots. `span_start`: A session's span starts at or after its window length and less than 8192 later.
All inputs are finite; a program needn't handle non-finite values.
Results may differ from a plain program's by a relative error of at most 0.04.
Values may be sent and summed in bfloat16 or wider, within the bound.
A program may use at most 128 MiB of HBM per device.

v0:
```python
import functools
import math

import jax
import jax.numpy as jnp
from jax import lax
from jax.experimental import pallas as pl
from jax.experimental.pallas import tpu as pltpu
from jax.sharding import PartitionSpec as P

QH = 32
KVH = 8
HD = 128


EPS = 1e-05
THETA = 500000.0
NEG = -1e30


def rotate(values, positions):
    half = values.shape[-1] // 2
    freq = THETA ** (-jnp.arange(half, dtype=jnp.float32) * 2.0 / values.shape[-1])
    angle = positions.astype(jnp.float32)[..., None] * freq
    cosine = jnp.cos(angle)[..., None, :]
    sine = jnp.sin(angle)[..., None, :]
    first = values[..., :half]
    second = values[..., half:]
    return jnp.concatenate(
        [first * cosine - second * sine, second * cosine + first * sine], axis=-1
    )


def body(gen_hidden, out_proj, norm_gain, q_weight, kv_weight, kv_cache, lengths, span_start):
    sessions, span, _ = gen_hidden.shape
    shards = lax.axis_size(("seq", "sub"))
    mine = lax.axis_index(("seq", "sub"))
    rows = span // shards
    local_heads = q_weight.shape[1] // HD
    group = QH // KVH
    scale = 1.0 / math.sqrt(HD)
    window_local = kv_cache.shape[2]
    summed = lax.psum(
        jnp.einsum("sci,id->csd", gen_hidden, out_proj, preferred_element_type=jnp.float32),
        ("seq", "sub"),
    )
    inputs = summed.astype(jnp.bfloat16)
    wide = inputs.astype(jnp.float32)
    inverse = lax.rsqrt(jnp.mean(wide * wide, axis=-1, keepdims=True) + EPS)
    normed = (wide * inverse * norm_gain.astype(jnp.float32)).astype(jnp.bfloat16)
    positions = span_start[None, :] + jnp.arange(span, dtype=jnp.int32)[:, None]
    query = jnp.einsum("csd,dh->csh", normed, q_weight, preferred_element_type=jnp.float32)
    query = rotate(query.reshape(span, sessions, local_heads, HD), positions).astype(jnp.bfloat16)
    kv_raw = jnp.einsum(
        "csd,jdk->jcsk", normed, kv_weight, preferred_element_type=jnp.float32
    ).astype(jnp.bfloat16)
    query_rows = jnp.arange(span, dtype=jnp.int32)
    new_rows = lax.all_to_all(kv_raw, ("seq", "sub"), split_axis=1, concat_axis=3, tiled=True)
    my_positions = lax.dynamic_slice_in_dim(positions, mine * rows, rows, 0)
    new_keys = rotate(
        new_rows[0].reshape(rows, sessions, KVH, HD).astype(jnp.float32), my_positions
    ).astype(jnp.bfloat16)
    new_values = new_rows[1].reshape(rows, sessions, KVH, HD)
    every_query = lax.all_gather(
        query.reshape(span, sessions, local_heads * HD), ("seq", "sub"), axis=2, tiled=True
    )
    grouped = every_query.reshape(span, sessions, KVH, group, HD)
    cached = kv_cache.reshape(2, sessions, window_local, KVH, HD)
    cache_scores = (
        jnp.einsum("csagh,swah->sagcw", grouped, cached[0], preferred_element_type=jnp.float32)
        * scale
    )
    slots = mine * window_local + jnp.arange(window_local, dtype=jnp.int32)
    live = slots[None, :] < lengths[:, None]
    cache_scores = jnp.where(live[:, None, None, None, :], cache_scores, NEG)
    span_scores = (
        jnp.einsum("csagh,tsah->sagct", grouped, new_keys, preferred_element_type=jnp.float32)
        * scale
    )
    key_rows = mine * rows + jnp.arange(rows, dtype=jnp.int32)
    causal = key_rows[None, :] <= query_rows[:, None]
    span_scores = jnp.where(causal, span_scores, NEG)
    top = jnp.maximum(jnp.max(cache_scores, axis=-1), jnp.max(span_scores, axis=-1))
    cache_weights = jnp.exp(cache_scores - top[..., None])
    span_weights = jnp.exp(span_scores - top[..., None])
    total = jnp.sum(cache_weights, axis=-1) + jnp.sum(span_weights, axis=-1)
    mixed = jnp.einsum(
        "sagcw,swah->scagh",
        cache_weights.astype(jnp.bfloat16),
        cached[1],
        preferred_element_type=jnp.float32,
    )
    mixed = mixed + jnp.einsum(
        "sagct,tsah->scagh",
        span_weights.astype(jnp.bfloat16),
        new_values,
        preferred_element_type=jnp.float32,
    )
    partial_value = mixed.reshape(1, sessions, span, QH * HD)
    peak = jnp.transpose(top, (0, 3, 1, 2)).reshape(1, sessions, span, QH)
    mass = jnp.transpose(total, (0, 3, 1, 2)).reshape(1, sessions, span, QH)
    pieces, peaks, masses = (
        lax.all_to_all(
            partial_value.astype(jnp.bfloat16),
            ("seq", "sub"),
            split_axis=2,
            concat_axis=0,
            tiled=True,
        ).astype(partial_value.dtype),
        lax.all_to_all(
            peak.astype(jnp.bfloat16), ("seq", "sub"), split_axis=2, concat_axis=0, tiled=True
        ).astype(peak.dtype),
        lax.all_to_all(
            mass.astype(jnp.bfloat16), ("seq", "sub"), split_axis=2, concat_axis=0, tiled=True
        ).astype(mass.dtype),
    )
    best = jnp.max(peaks, axis=0)
    factor = jnp.exp(peaks - best[None])
    numer = jnp.sum(factor[..., None] * pieces.reshape(shards, sessions, rows, QH, HD), axis=0)
    denom = jnp.sum(factor * masses, axis=0)
    return (numer / denom[..., None]).astype(jnp.bfloat16).reshape(sessions, rows, QH * HD)


MESH = pl.DeviceIdType.MESH
CHUNKS = 2
BF = jnp.bfloat16
F32 = jnp.float32


def fused_kernel(
    shards_z,
    hid,
    wo,
    gain,
    wq,
    wkv,
    cache,
    lengths,
    starts,
    freqs,
    out,
    hid_v,
    wo_v,
    w_v,
    k_v,
    v_v,
    p_send,
    p_recv,
    own_part,
    rs_send,
    rs_recv,
    rs_merged,
    x_all,
    acc,
    ssq,
    q_all,
    kn,
    vn,
    o_send,
    o_recv,
    o_merged,
    fin,
    f_recv,
    rope_v,
    in_sem,
    wo_sem,
    kvl_sem,
    kvs_sem,
    kvr_sem,
    ps_sem,
    pr_sem,
    rss_sem,
    rsr_sem,
    ags_sem,
    agr_sem,
    fws_sem,
    fwr_sem,
    qs_sem,
    qr_sem,
    os_sem,
    or_sem,
    fs_sem,
    fr_sem,
):
    Z = shards_z
    z = lax.axis_index("seq")
    c = lax.axis_index("sub")
    other = 1 - c
    rows = hid.shape[2]
    span = 2 * Z * rows
    width = wo.shape[1]
    cw = width // CHUNKS
    ql = wq.shape[1]
    heads = ql // HD
    wl = cache.shape[1]
    tile = 256
    partner = {"seq": z, "sub": other}

    inner = (z == 1) | (z == 2)
    near = z + 1 - 2 * lax.rem(z, 2)
    far_in = jnp.where(z < 2, 2, 1)
    far_out = jnp.where(z < 2, 3, 0)
    group_at = (z, near, far_in, far_out)
    my_in = jnp.where(z < 2, 1, 2)
    my_out = jnp.where(z < 2, 0, 3)
    merge_order = (my_out, my_in, far_in, far_out)

    def remote(src, dst, ss, rs, zz, cc):
        return pltpu.make_async_remote_copy(
            src_ref=src,
            dst_ref=dst,
            send_sem=ss,
            recv_sem=rs,
            device_id={"seq": zz, "sub": cc},
            device_id_type=MESH,
        )

    def hid_copy():
        return (
            pltpu.make_async_copy(hid.at[:, other], hid_v.at[0], in_sem.at[0]),
            pltpu.make_async_copy(hid.at[:, c], hid_v.at[1], in_sem.at[4]),
        )

    def wo_copy(k):
        return pltpu.make_async_copy(
            wo.at[:, pl.ds(pl.multiple_of(k * cw, cw), cw)], wo_v.at[k], wo_sem.at[k]
        )

    def w_copies():
        return (
            pltpu.make_async_copy(wq, w_v.at[:, 0:ql], in_sem.at[1]),
            pltpu.make_async_copy(wkv.at[0], w_v.at[:, ql : ql + HD], in_sem.at[2]),
            pltpu.make_async_copy(wkv.at[1], w_v.at[:, ql + HD : ql + 2 * HD], in_sem.at[3]),
        )

    def kv_src(i, j, cc):
        return cache.at[i, :, pl.ds(pl.multiple_of((2 * j + cc) * HD, HD), HD)]

    def kv_dst(i, j):
        return (k_v, v_v)[i].at[j, pl.ds(pl.multiple_of(c * wl, wl), wl), :]

    def kv_local(i, j):
        return pltpu.make_async_copy(kv_src(i, j, c), kv_dst(i, j), kvl_sem.at[i, j])

    def kv_remote(i, j):
        return remote(
            kv_src(i, j, other), kv_dst(i, j), kvs_sem.at[i, j], kvr_sem.at[i, j], z, other
        )

    def pair_copy(k):
        return remote(p_send.at[k], p_recv.at[k], ps_sem.at[k], pr_sem.at[k], z, other)

    mine = 2 * z + c

    def rs_copy(k, slot, who):
        return remote(
            rs_send.at[k, who],
            rs_recv.at[k, slot],
            rss_sem.at[k, slot],
            rsr_sem.at[k, slot],
            near,
            c,
        )

    def rs_cross(k, which):
        who = (far_in, far_out)[which]
        return remote(
            rs_merged.at[k, which],
            rs_recv.at[k, 4],
            rss_sem.at[k, 4 + which],
            rsr_sem.at[k, 4],
            who,
            c,
        )

    def ag_copy(k, block, slot, sem, who):
        blk = x_all.at[k, 2 * block + c]
        return remote(blk, blk, ags_sem.at[k, sem], agr_sem.at[k, slot], who, c)

    def fw_copy(k, d):
        blk = x_all.at[k, 2 * group_at[d] + c]
        return remote(blk, blk, fws_sem.at[k, d], fwr_sem.at[k, d], z, other)

    def q_copy(block, slot, sem, who):
        blk = q_all.at[block]
        return remote(blk, blk, qs_sem.at[sem], qr_sem.at[slot], who, c)

    def chip_rows(who):
        return pl.ds(pl.multiple_of(who * 2 * rows, 2 * rows), 2 * rows)

    def o_copy(j, slot, who):
        return remote(
            o_send.at[j, chip_rows(who), :],
            o_recv.at[slot, j],
            os_sem.at[j, slot],
            or_sem.at[j, slot],
            near,
            c,
        )

    def o_cross(j, which):
        who = (far_in, far_out)[which]
        return remote(
            o_merged.at[j, which],
            o_recv.at[4, j],
            os_sem.at[j, 4 + which],
            or_sem.at[j, 4],
            who,
            c,
        )

    def f_copy():
        src = fin.at[:, pl.ds(pl.multiple_of(other * rows, rows), rows), :]
        return remote(src, f_recv, fs_sem.at[0], fr_sem.at[0], z, other)

    for copy in hid_copy():
        copy.start()
    for k in range(CHUNKS):
        wo_copy(k).start()
    barrier = pltpu.get_barrier_semaphore()
    for who in (near, far_in, far_out):
        pl.semaphore_signal(
            barrier, inc=1, device_id={"seq": who, "sub": c}, device_id_type=MESH
        )
    pl.semaphore_signal(barrier, inc=1, device_id=partner, device_id_type=MESH)
    pl.semaphore_wait(barrier, Z)

    for copy in hid_copy():
        copy.wait()
    ssq[...] = jnp.zeros_like(ssq)
    acc[...] = jnp.zeros_like(acc)

    def pair_sum(k):
        pair_copy(k).wait_recv()
        both = own_part[k] + p_recv[k].astype(F32)
        rs_send[k] = both.astype(BF).reshape(Z, rows, cw)
        @pl.when(jnp.logical_not(inner))
        def _():
            rs_copy(k, 3, far_out).start()
            rs_copy(k, 2, far_in).start()

        rs_copy(k, 1, near).start()

    def stage_a(k, carry):
        wo_copy(k).wait()

        lhs = hid_v[...].reshape(span, hid.shape[3])
        half = Z * rows

        def go(t, carry):
            cols = pl.ds(pl.multiple_of(t * tile, tile), tile)
            value = jnp.dot(lhs, wo_v[k, :, cols], preferred_element_type=F32)
            p_send[k, :, cols] = value[:half].astype(BF)
            own_part[k, :, cols] = value[half:]
            return carry

        lax.fori_loop(0, cw // tile, go, 0)
        pair_copy(k).start()

        @pl.when(k >= 1)
        def _():
            pair_sum(k - 1)

        return carry

    lax.fori_loop(0, CHUNKS, stage_a, 0)
    pair_sum(CHUNKS - 1)

    for copy in w_copies():
        copy.start()
    for i in range(2):
        for j in range(Z):
            kv_local(i, j).start()
            kv_remote(i, j).start()

    def merge_rs(k):
        for which, who in ((1, far_out), (0, far_in)):
            rs_copy(k, 2 + which, who).wait_recv()
            both = rs_send[k, who].astype(F32) + rs_recv[k, 2 + which].astype(F32)
            rs_merged[k, which] = both.astype(BF)
            rs_cross(k, which).start()

    def stage_c(k):
        total = rs_send[k, z].astype(F32)
        rs_copy(k, 1, near).wait_recv()
        total = total + rs_recv[k, 1].astype(F32)
        rs_cross(k, 0).wait_recv()
        total = total + rs_recv[k, 4].astype(F32)
        x_all[k, mine] = total.astype(BF)
        ag_copy(k, z, 1, 0, near).start()

        @pl.when(inner)
        def _():
            ag_copy(k, z, 2, 1, far_in).start()

        fw_copy(k, 0).start()

    def ag_wait(k, slot):
        ag_copy(k, group_at[slot], slot, 0, near).wait_recv()

    def fw_wait(k, d):
        blk = x_all.at[k, 2 * group_at[d] + other]
        remote(blk, blk, fws_sem.at[k, d], fwr_sem.at[k, d], z, other).wait_recv()

    def stage_d(k):
        ag_wait(k, 1)
        fw_copy(k, 1).start()

        @pl.when(inner)
        def _():
            ag_copy(k, near, 3, 2, far_in).start()

        ag_wait(k, 2)
        fw_copy(k, 2).start()

        @pl.when(inner)
        def _():
            ag_copy(k, far_in, 2, 3, near).start()

        ag_wait(k, 3)
        fw_copy(k, 3).start()

        @pl.when(inner)
        def _():
            ag_copy(k, far_out, 3, 4, near).start()

    def stage_e(k):
        for d in range(Z):
            fw_wait(k, d)
        x = x_all[k].reshape(span, cw).astype(F32)
        ssq[...] += jnp.sum(x * x, axis=-1, keepdims=True)
        cols = pl.ds(pl.multiple_of(k * cw, cw), cw)
        xg = (x * gain[cols].astype(F32).reshape(1, cw)).astype(BF)
        acc[...] += jnp.dot(xg, w_v[cols, :], preferred_element_type=F32)

    def staggered(step, carry):
        @pl.when(inner & (step < CHUNKS))
        def _():
            merge_rs(step)

        @pl.when((step >= 1) & (step < CHUNKS + 1))
        def _():
            stage_c(step - 1)

        @pl.when((step >= 2) & (step < CHUNKS + 2))
        def _():
            stage_d(step - 2)

        @pl.when(step == 3)
        def _():
            for copy in w_copies():
                copy.wait()

        @pl.when(step >= 3)
        def _():
            stage_e(step - 3)

        return carry

    angle = (starts[0] + lax.broadcasted_iota(jnp.int32, (span, HD), 0)).astype(F32) * freqs[...]
    rope_v[0] = jnp.cos(angle)
    sines = jnp.sin(angle)
    first = lax.broadcasted_iota(jnp.int32, (span, HD), 1) < HD // 2
    rope_v[1] = jnp.where(first, -sines, sines)

    lax.fori_loop(0, CHUNKS + 3, staggered, 0)

    inverse = lax.rsqrt(ssq[...] * (1.0 / width) + EPS)
    cosine = rope_v[0]
    sine = rope_v[1]

    def rope(value):
        return value * cosine + pltpu.roll(value, HD // 2, 1) * sine

    for h in range(heads):
        value = acc[:, h * HD : (h + 1) * HD] * inverse
        q_all[z, :, h * HD : (h + 1) * HD] = rope(value).astype(BF)
    q_copy(z, 1, 0, near).start()

    @pl.when(inner)
    def _():
        q_copy(z, 2, 1, far_in).start()

    key_raw = (acc[:, ql : ql + HD] * inverse).astype(BF)
    kn[...] = rope(key_raw.astype(F32)).astype(BF)
    vn[...] = (acc[:, ql + HD : ql + 2 * HD] * inverse).astype(BF)

    for i in range(2):
        for j in range(Z):
            kv_local(i, j).wait()
            kv_remote(i, j).wait_recv()

    length = lengths[0]
    slots = z * 2 * wl + lax.broadcasted_iota(jnp.int32, (1, 2 * wl), 1)
    live = slots < length
    c2 = math.log2(math.e) / math.sqrt(HD)
    nt = (((1,), (1,)), ((), ()))
    lane = lax.broadcasted_iota(jnp.int32, (span, HD), 1)

    def packed_stats(stats, count):
        high = stats.astype(BF).astype(F32)
        lanes = lax.broadcasted_iota(jnp.int32, (count, HD), 1)
        return jnp.where(lanes < heads, high, stats - high).astype(BF)

    def attend(j, own):
        def head(h, stats):
            cols = pl.ds(pl.multiple_of(h * HD, HD), HD)
            q = q_all[j, :, cols]
            s = lax.dot_general(q, k_v[j], nt, preferred_element_type=F32)
            s = jnp.where(live, s, NEG)
            top = jnp.max(s, axis=-1, keepdims=True)
            if own:
                s2 = lax.dot_general(q, kn[...], nt, preferred_element_type=F32)
                r = lax.broadcasted_iota(jnp.int32, (span, span), 0)
                t = lax.broadcasted_iota(jnp.int32, (span, span), 1)
                s2 = jnp.where(t <= r, s2, NEG)
                top = jnp.maximum(top, jnp.max(s2, axis=-1, keepdims=True))
            top = top * c2
            p = jnp.exp2(s * c2 - top)
            total = jnp.sum(p, axis=-1, keepdims=True)
            mixed = jnp.dot(p.astype(BF), v_v[j], preferred_element_type=F32)
            if own:
                p2 = jnp.exp2(s2 * c2 - top)
                total = total + jnp.sum(p2, axis=-1, keepdims=True)
                mixed = mixed + jnp.dot(p2.astype(BF), vn[...], preferred_element_type=F32)
            o_send[j, :, cols] = (mixed * (1.0 / total)).astype(BF)
            lse = top + jnp.log2(total)
            return jnp.where((lane == h) | (lane == h + heads), lse, stats)

        stats = lax.fori_loop(0, heads, head, jnp.zeros((span, HD), F32))
        o_send[j, :, ql : ql + HD] = packed_stats(stats, span)
        @pl.when(jnp.logical_not(inner))
        def _():
            o_copy(j, 3, far_out).start()
            o_copy(j, 2, far_in).start()

        o_copy(j, 1, near).start()

    def joined(parts):
        stats = []
        for p in parts:
            both = p[:, ql : ql + HD].astype(F32)
            stats.append(both + pltpu.roll(both, HD - heads, 1))
        best = functools.reduce(jnp.maximum, stats)
        shares = [jnp.exp2(s - best) for s in stats]
        total = functools.reduce(lambda a, b: a + b, shares)
        inv = 1.0 / total
        shares = [s * inv for s in shares]
        mixes = []
        for h in range(heads):
            cols = slice(h * HD, (h + 1) * HD)
            terms = [s[:, h : h + 1] * p[:, cols].astype(F32) for s, p in zip(shares, parts)]
            mixes.append(functools.reduce(lambda a, b: a + b, terms).astype(BF))
        return mixes, best + jnp.log2(total)

    def merge_o(j):
        for which, who in ((1, far_out), (0, far_in)):
            o_copy(j, 2 + which, who).wait_recv()
            mixes, lse = joined((o_send[j, chip_rows(who), :], o_recv[2 + which, j]))
            for h in range(heads):
                o_merged[j, which, :, h * HD : (h + 1) * HD] = mixes[h]
            low = lax.broadcasted_iota(jnp.int32, lse.shape, 1) < heads
            lse = jnp.where(low, lse, pltpu.roll(lse, heads, 1))
            o_merged[j, which, :, ql : ql + HD] = packed_stats(lse, 2 * rows)
            o_cross(j, which).start()

    attend(z, True)

    def q_wait(slot):
        q_copy(group_at[slot], slot, 0, near).wait_recv()

    q_wait(1)

    @pl.when(inner)
    def _():
        q_copy(near, 3, 2, far_in).start()

    def attend_others(slot, carry):
        j = jnp.where(slot == 1, near, jnp.where(slot == 2, far_in, far_out))

        @pl.when(slot >= 2)
        def _():
            blk = q_all.at[j]
            remote(blk, blk, qs_sem.at[0], qr_sem.at[slot], near, c).wait_recv()

            @pl.when(inner)
            def _():
                remote(blk, blk, qs_sem.at[slot + 1], qr_sem.at[slot], near, c).start()

        attend(j, False)

        @pl.when(inner)
        def _():
            merge_o(jnp.where(slot == 1, my_out, jnp.where(slot == 2, my_in, far_in)))

        return carry

    lax.fori_loop(1, Z, attend_others, 0)

    @pl.when(inner)
    def _():
        merge_o(far_out)

    def combine(j, carry):
        o_copy(j, 1, near).wait_recv()
        o_cross(j, 0).wait_recv()
        mixes, _ = joined((o_send[j, chip_rows(z), :], o_recv[1, j], o_recv[4, j]))
        for h in range(heads):
            fin[j, :, h * HD : (h + 1) * HD] = mixes[h]
        return carry

    lax.fori_loop(0, Z, combine, 0)
    f_copy().start()
    keep = pl.ds(pl.multiple_of(c * rows, rows), rows)
    for j in range(Z):
        out[0, :, pl.ds(pl.multiple_of((2 * j + c) * ql, ql), ql)] = fin[j, keep, :]
    f_copy().wait_recv()
    for j in range(Z):
        out[0, :, pl.ds(pl.multiple_of((2 * j + other) * ql, ql), ql)] = f_recv[j]

    f_copy().wait_send()
    for i in range(2):
        for j in range(Z):
            kv_remote(i, j).wait_send()

    outer = jnp.logical_not(inner)

    def drain(k, carry):
        pair_copy(k).wait_send()
        rs_copy(k, 1, near).wait_send()
        ag_copy(k, z, 1, 0, near).wait_send()
        for d in range(Z):
            fw_copy(k, d).wait_send()

        @pl.when(outer)
        def _():
            rs_copy(k, 2, far_in).wait_send()
            rs_copy(k, 3, far_out).wait_send()

        @pl.when(inner)
        def _():
            rs_cross(k, 0).wait_send()
            rs_cross(k, 1).wait_send()
            ag_copy(k, z, 2, 1, far_in).wait_send()
            ag_copy(k, near, 3, 2, far_in).wait_send()
            ag_copy(k, far_in, 2, 3, near).wait_send()
            ag_copy(k, far_out, 3, 4, near).wait_send()

        return carry

    lax.fori_loop(0, CHUNKS, drain, 0)
    q_copy(z, 1, 0, near).wait_send()

    @pl.when(inner)
    def _():
        q_copy(z, 2, 1, far_in).wait_send()
        q_copy(near, 3, 2, far_in).wait_send()
        q_copy(far_in, 2, 3, near).wait_send()
        q_copy(far_out, 3, 4, near).wait_send()

    def drain_o(j, carry):
        o_copy(j, 1, near).wait_send()

        @pl.when(outer)
        def _():
            o_copy(j, 2, far_in).wait_send()
            o_copy(j, 3, far_out).wait_send()

        @pl.when(inner)
        def _():
            o_cross(j, 0).wait_send()
            o_cross(j, 1).wait_send()

        return carry

    lax.fori_loop(0, Z, drain_o, 0)


def fused(gen_hidden, out_proj, norm_gain, q_weight, kv_weight, kv_cache, lengths, span_start):
    Z = lax.axis_size("seq")
    _, span, dl = gen_hidden.shape
    rows = span // (2 * Z)
    width = out_proj.shape[1]
    cw = width // CHUNKS
    ql = q_weight.shape[1]
    wl = kv_cache.shape[2]
    half = HD // 2
    freq = THETA ** (-jnp.arange(half, dtype=F32) * 2.0 / HD)
    freqs = jnp.concatenate([freq, freq])[None, :]
    any_spec = pl.BlockSpec(memory_space=pl.ANY)
    vm_spec = pl.BlockSpec(memory_space=pltpu.VMEM)
    sm_spec = pl.BlockSpec(memory_space=pltpu.SMEM)
    dma = pltpu.SemaphoreType.DMA
    V = pltpu.VMEM
    return pl.pallas_call(
        functools.partial(fused_kernel, Z),
        out_shape=jax.ShapeDtypeStruct((1, rows, 2 * Z * ql), BF),
        in_specs=[any_spec, any_spec, vm_spec, any_spec, any_spec, any_spec, sm_spec, sm_spec, vm_spec],
        out_specs=vm_spec,
        scratch_shapes=[
            V((2, Z, rows, dl), BF),
            V((CHUNKS, dl, cw), BF),
            V((width, ql + 2 * HD), BF),
            V((Z, 2 * wl, HD), BF),
            V((Z, 2 * wl, HD), BF),
            V((CHUNKS, Z * rows, cw), BF),
            V((CHUNKS, Z * rows, cw), BF),
            V((CHUNKS, Z * rows, cw), F32),
            V((CHUNKS, Z, rows, cw), BF),
            V((CHUNKS, Z + 1, rows, cw), BF),
            V((CHUNKS, 2, rows, cw), BF),
            V((CHUNKS, 2 * Z, rows, cw), BF),
            V((span, ql + 2 * HD), F32),
            V((span, 1), F32),
            V((Z, span, ql), BF),
            V((span, HD), BF),
            V((span, HD), BF),
            V((Z, span, ql + HD), BF),
            V((Z + 1, Z, 2 * rows, ql + HD), BF),
            V((Z, 2, 2 * rows, ql + HD), BF),
            V((Z, 2 * rows, ql), BF),
            V((Z, rows, ql), BF),
            V((2, span, HD), F32),
            dma((5,)),
            dma((CHUNKS,)),
            dma((2, Z)),
            dma((2, Z)),
            dma((2, Z)),
            dma((CHUNKS,)),
            dma((CHUNKS,)),
            dma((CHUNKS, 6)),
            dma((CHUNKS, 5)),
            dma((CHUNKS, 5)),
            dma((CHUNKS, Z)),
            dma((CHUNKS, Z)),
            dma((CHUNKS, Z)),
            dma((5,)),
            dma((Z,)),
            dma((Z, 6)),
            dma((Z, 5)),
            dma((1,)),
            dma((1,)),
        ],
        compiler_params=pltpu.CompilerParams(
            collective_id=0, has_side_effects=True, vmem_limit_bytes=64000000
        ),
    )(
        gen_hidden.reshape(Z, 2, rows, dl),
        out_proj,
        norm_gain,
        q_weight,
        kv_weight,
        kv_cache.reshape(2, wl, KVH * HD),
        lengths,
        span_start,
        freqs,
    )


def solution(mesh):
    placed = (
        P(("groups", "batch"), None, ("seq", "sub")),
        P(("seq", "sub"), None),
        P(),
        P(None, ("seq", "sub")),
        P(None, None, ("seq", "sub")),
        P(None, ("groups", "batch"), ("seq", "sub"), None),
        P(("groups", "batch")),
        P(("groups", "batch")),
    )
    aligned = mesh.shape["sub"] == 2 and mesh.shape["seq"] * 2 == KVH
    return jax.shard_map(
        fused if aligned else body,
        mesh=mesh,
        in_specs=placed,
        out_specs=P(("groups", "batch"), ("seq", "sub"), None),
        check_vma=False,
    )
```

profile of v0, /device:TPU:28, one launch (start us, length us, event | category | flops | bytes accessed | tf_op | source)
XLA Modules:
  0.0 102.3 jit_solution(628250174684530463)
XLA Ops:
  1.3 0.6 maximum_bitcast_fusion.freqs
  1.9 98.7 %shard_map.82 = bf16[1,32,4096]{2,1,0:T(8,128)(2,1)} custom-call(bf16[4,2,32,1024]{3,2,1,0:T(8,128)(2,1)} %bitcast.5, bf16[1024,4096]{1,0:T(8,128)(2,1)} %wo.1, bf16[4096]{0:T(1024)(128)(2,1)} %gain.1, bf16[4096,512]{1,0:T(8,128)(2,1)} %wq.1, bf16[2,4096,128]{2,1,0:T(8,128)(2,1)} %wkv.1, bf16[2,1024,1024]{2,1,0:T(8,128)(2,1)} %bitcast.4, ...), custom_call_target="tpu_custom_call" | custom-call | tf_op jit(solution)/shard_map/pallas_call | solution.py:695
  100.6 1.7 %copy.12 = bf16[1,32,4096]{2,1,0:T(8,128)(2,1)} copy(bf16[1,32,4096]{2,1,0:T(8,128)(2,1)} %shard_map.82) | data formatting | bytes 524288
  (1 shorter events, 0.0 us)
where the time goes:
time: 104 us; the launch traced here: 102 us
  Pallas kernels  98.7 us (95%)
  local copies, waits for them, and re-layouts  1.67 us (2%)
  between operations  1.31 us (1%)
    pallas_call x1, Pallas kernels, fused(): pl.pallas_call(functools.partial(fused_kernel, Z), out_shape=jax.ShapeDty...  98.7 us

commit v1 on v0

v1 whole, which is shorter than its diff:
```python
import functools
import math

import jax
import jax.numpy as jnp
import numpy as np
from jax import lax
from jax.experimental import pallas as pl
from jax.experimental.pallas import tpu as pltpu
from jax.sharding import PartitionSpec as P

QH = 32
KVH = 8
HD = 128


EPS = 1e-05
THETA = 500000.0
NEG = -1e30


def rotate(values, positions):
    half = values.shape[-1] // 2
    freq = THETA ** (-jnp.arange(half, dtype=jnp.float32) * 2.0 / values.shape[-1])
    angle = positions.astype(jnp.float32)[..., None] * freq
    cosine = jnp.cos(angle)[..., None, :]
    sine = jnp.sin(angle)[..., None, :]
    first = values[..., :half]
    second = values[..., half:]
    return jnp.concatenate(
        [first * cosine - second * sine, second * cosine + first * sine], axis=-1
    )


def body(gen_hidden, out_proj, norm_gain, q_weight, kv_weight, kv_cache, lengths, span_start):
    sessions, span, _ = gen_hidden.shape
    shards = lax.axis_size(("seq", "sub"))
    mine = lax.axis_index(("seq", "sub"))
    rows = span // shards
    local_heads = q_weight.shape[1] // HD
    group = QH // KVH
    scale = 1.0 / math.sqrt(HD)
    window_local = kv_cache.shape[2]
    summed = lax.psum(
        jnp.einsum("sci,id->csd", gen_hidden, out_proj, preferred_element_type=jnp.float32),
        ("seq", "sub"),
    )
    inputs = summed.astype(jnp.bfloat16)
    wide = inputs.astype(jnp.float32)
    inverse = lax.rsqrt(jnp.mean(wide * wide, axis=-1, keepdims=True) + EPS)
    normed = (wide * inverse * norm_gain.astype(jnp.float32)).astype(jnp.bfloat16)
    positions = span_start[None, :] + jnp.arange(span, dtype=jnp.int32)[:, None]
    query = jnp.einsum("csd,dh->csh", normed, q_weight, preferred_element_type=jnp.float32)
    query = rotate(query.reshape(span, sessions, local_heads, HD), positions).astype(jnp.bfloat16)
    kv_raw = jnp.einsum(
        "csd,jdk->jcsk", normed, kv_weight, preferred_element_type=jnp.float32
    ).astype(jnp.bfloat16)
    query_rows = jnp.arange(span, dtype=jnp.int32)
    new_rows = lax.all_to_all(kv_raw, ("seq", "sub"), split_axis=1, concat_axis=3, tiled=True)
    my_positions = lax.dynamic_slice_in_dim(positions, mine * rows, rows, 0)
    new_keys = rotate(
        new_rows[0].reshape(rows, sessions, KVH, HD).astype(jnp.float32), my_positions
    ).astype(jnp.bfloat16)
    new_values = new_rows[1].reshape(rows, sessions, KVH, HD)
    every_query = lax.all_gather(
        query.reshape(span, sessions, local_heads * HD), ("seq", "sub"), axis=2, tiled=True
    )
    grouped = every_query.reshape(span, sessions, KVH, group, HD)
    cached = kv_cache.reshape(2, sessions, window_local, KVH, HD)
    cache_scores = (
        jnp.einsum("csagh,swah->sagcw", grouped, cached[0], preferred_element_type=jnp.float32)
        * scale
    )
    slots = mine * window_local + jnp.arange(window_local, dtype=jnp.int32)
    live = slots[None, :] < lengths[:, None]
    cache_scores = jnp.where(live[:, None, None, None, :], cache_scores, NEG)
    span_scores = (
        jnp.einsum("csagh,tsah->sagct", grouped, new_keys, preferred_element_type=jnp.float32)
        * scale
    )
    key_rows = mine * rows + jnp.arange(rows, dtype=jnp.int32)
    causal = key_rows[None, :] <= query_rows[:, None]
    span_scores = jnp.where(causal, span_scores, NEG)
    top = jnp.maximum(jnp.max(cache_scores, axis=-1), jnp.max(span_scores, axis=-1))
    cache_weights = jnp.exp(cache_scores - top[..., None])
    span_weights = jnp.exp(span_scores - top[..., None])
    total = jnp.sum(cache_weights, axis=-1) + jnp.sum(span_weights, axis=-1)
    mixed = jnp.einsum(
        "sagcw,swah->scagh",
        cache_weights.astype(jnp.bfloat16),
        cached[1],
        preferred_element_type=jnp.float32,
    )
    mixed = mixed + jnp.einsum(
        "sagct,tsah->scagh",
        span_weights.astype(jnp.bfloat16),
        new_values,
        preferred_element_type=jnp.float32,
    )
    partial_value = mixed.reshape(1, sessions, span, QH * HD)
    peak = jnp.transpose(top, (0, 3, 1, 2)).reshape(1, sessions, span, QH)
    mass = jnp.transpose(total, (0, 3, 1, 2)).reshape(1, sessions, span, QH)
    pieces, peaks, masses = (
        lax.all_to_all(
            partial_value.astype(jnp.bfloat16),
            ("seq", "sub"),
            split_axis=2,
            concat_axis=0,
            tiled=True,
        ).astype(partial_value.dtype),
        lax.all_to_all(
            peak.astype(jnp.bfloat16), ("seq", "sub"), split_axis=2, concat_axis=0, tiled=True
        ).astype(peak.dtype),
        lax.all_to_all(
            mass.astype(jnp.bfloat16), ("seq", "sub"), split_axis=2, concat_axis=0, tiled=True
        ).astype(mass.dtype),
    )
    best = jnp.max(peaks, axis=0)
    factor = jnp.exp(peaks - best[None])
    numer = jnp.sum(factor[..., None] * pieces.reshape(shards, sessions, rows, QH, HD), axis=0)
    denom = jnp.sum(factor * masses, axis=0)
    return (numer / denom[..., None]).astype(jnp.bfloat16).reshape(sessions, rows, QH * HD)


MESH = pl.DeviceIdType.MESH
BF = jnp.bfloat16
F32 = jnp.float32
TILE = 512
LEFT, FULL, QKV, ATTEND, MERGE, PASS, NEED_W, NEED_KV = range(1, 9)
CHUNKS = 4
ORDER = (0, 3, 2, 1)
PLAN = (
    (
        128, 136, 144, 152, 131, 448, 192, 512, 256, 139, 257, 147, 258, 155, 130, 216,
        281, 138, 146, 154, 208, 129, 282, 273, 137, 145, 153, 200, 280, 272, 322, 274,
        264, 265, 321, 283, 259, 323, 266, 275, 267, 320, 0, 0, 0, 0, 0, 0,
        0, 0, 0, 0, 0, 0, 0, 0, 0, 0, 0, 0, 0, 0, 0, 0,
        0, 0, 0, 0, 0, 0, 0, 0, 0, 0, 0, 0, 0, 0, 0, 0,
        0, 0,
    ),
    (
        64, 72, 80, 128, 88, 136, 67, 144, 75, 152, 83, 131, 448, 192, 91, 66,
        139, 512, 257, 74, 147, 386, 258, 82, 155, 90, 130, 216, 65, 73, 138, 146,
        81, 154, 89, 410, 282, 384, 129, 208, 137, 408, 256, 145, 280, 153, 387, 259,
        200, 400, 402, 281, 322, 323, 345, 346, 273, 321, 411, 337, 283, 394, 272, 403,
        392, 274, 275, 344, 265, 395, 336, 264, 320, 338, 266, 267, 347, 330, 339, 329,
        331, 328,
    ),
    (
        64, 72, 80, 128, 88, 136, 67, 144, 75, 152, 83, 131, 448, 192, 91, 66,
        139, 512, 258, 74, 147, 385, 257, 82, 155, 90, 130, 216, 65, 73, 138, 146,
        81, 154, 89, 409, 281, 387, 129, 208, 137, 259, 145, 322, 323, 153, 321, 384,
        256, 411, 401, 200, 408, 403, 282, 283, 393, 280, 400, 266, 345, 265, 346, 274,
        395, 267, 392, 320, 264, 275, 273, 344, 337, 331, 272, 336, 338, 330, 329, 347,
        328, 339,
    ),
    (
        128, 136, 144, 152, 131, 448, 192, 512, 259, 139, 258, 147, 257, 155, 130, 216,
        282, 138, 146, 154, 208, 129, 281, 274, 137, 145, 153, 200, 256, 275, 273, 267,
        272, 266, 345, 265, 346, 283, 264, 280, 344, 347, 0, 0, 0, 0, 0, 0,
        0, 0, 0, 0, 0, 0, 0, 0, 0, 0, 0, 0, 0, 0, 0, 0,
        0, 0, 0, 0, 0, 0, 0, 0, 0, 0, 0, 0, 0, 0, 0, 0,
        0, 0,
    ),
)


def packed_plan(steps):
    steps = list(steps) + [0] * (-len(steps) % 3)
    return [a + 1024 * b + 1048576 * c for a, b, c in zip(*[iter(steps)] * 3)]


def fused_kernel(
    shards_z,
    hid,
    wo,
    gain,
    wq,
    wkv,
    cache,
    lengths,
    starts,
    freqs,
    out,
    hid_v,
    wo_v,
    w_v,
    k_v,
    v_v,
    p_send,
    p_recv,
    own_part,
    part,
    part_in,
    side,
    side_in,
    x_all,
    xg_v,
    q_all,
    kn,
    vn,
    o_loc,
    o_in,
    f_recv,
    rope_v,
    in_sem,
    wo_sem,
    kvl_sem,
    kvs_sem,
    kvr_sem,
    ps_sem,
    pr_sem,
    outs_sem,
    outr_sem,
    mids_sem,
    midr_sem,
    xs_sem,
    xr_sem,
    fws_sem,
    fwr_sem,
    qs_sem,
    qr_sem,
    os_sem,
    or_sem,
    fs_sem,
    fr_sem,
):
    Z = shards_z
    z = lax.axis_index("seq")
    c = lax.axis_index("sub")
    other = 1 - c
    rows = hid.shape[2]
    pair = 2 * rows
    span = Z * pair
    width = wo.shape[1]
    cw = width // CHUNKS
    ql = wq.shape[1]
    heads = ql // HD
    stack = heads * pair
    wl = cache.shape[1]

    inner = (z == 1) | (z == 2)
    outer = jnp.logical_not(inner)
    near = z + 1 - 2 * lax.rem(z, 2)
    far_in = jnp.where(z < 2, 2, 1)

    def remote(src, dst, ss, rs, zz, cc):
        return pltpu.make_async_remote_copy(
            src_ref=src,
            dst_ref=dst,
            send_sem=ss,
            recv_sem=rs,
            device_id={"seq": zz, "sub": cc},
            device_id_type=MESH,
        )

    def hid_copy():
        return (
            pltpu.make_async_copy(hid.at[:, other], hid_v.at[0], in_sem.at[0]),
            pltpu.make_async_copy(hid.at[:, c], hid_v.at[1], in_sem.at[4]),
        )

    def wo_copy(k):
        return pltpu.make_async_copy(
            wo.at[:, pl.ds(pl.multiple_of(k * cw, cw), cw)], wo_v.at[k], wo_sem.at[k]
        )

    def w_copies():
        return (
            pltpu.make_async_copy(wq, w_v.at[:, 0:ql], in_sem.at[1]),
            pltpu.make_async_copy(wkv.at[0], w_v.at[:, ql : ql + HD], in_sem.at[2]),
            pltpu.make_async_copy(wkv.at[1], w_v.at[:, ql + HD : ql + 2 * HD], in_sem.at[3]),
        )

    def kv_src(i, j, cc):
        return cache.at[i, :, pl.ds(pl.multiple_of((2 * j + cc) * HD, HD), HD)]

    def kv_dst(i, j):
        return (k_v, v_v)[i].at[j, pl.ds(pl.multiple_of(c * wl, wl), wl), :]

    def kv_local(i, j):
        return pltpu.make_async_copy(kv_src(i, j, c), kv_dst(i, j), kvl_sem.at[i, j])

    def kv_remote(i, j):
        return remote(
            kv_src(i, j, other), kv_dst(i, j), kvs_sem.at[i, j], kvr_sem.at[i, j], z, other
        )

    def pair_copy(k):
        return remote(p_send.at[k], p_recv.at[k], ps_sem.at[k], pr_sem.at[k], z, other)

    def out_copy(k, r):
        return remote(part.at[k, r], part_in.at[k, r], outs_sem.at[k, r], outr_sem.at[k, r], near, c)

    def mid_copy(k, r):
        return remote(
            side.at[k, r], side_in.at[k, r], mids_sem.at[k, r], midr_sem.at[k, r], far_in, c
        )

    def x_copy(k, r):
        blk = x_all.at[k, 2 * r + c]
        return remote(blk, blk, xs_sem.at[k, r], xr_sem.at[k, r], near, c)

    def fw_copy(k, r, core):
        blk = x_all.at[k, 2 * r + core]
        return remote(blk, blk, fws_sem.at[k, r], fwr_sem.at[k, r], z, other)

    def q_copy(r, j, sem, who):
        blk = q_all.at[r, j]
        return remote(blk, blk, qs_sem.at[r, sem], qr_sem.at[r, j], who, c)

    def o_copy(r, j):
        up = jnp.where(z < r, 0, 1)
        who = jnp.where(z < r, z + 1, z - 1)
        return remote(
            o_loc.at[r, j], o_in.at[r, j, up], os_sem.at[r, j], or_sem.at[r, j, up], who, c
        )

    def f_copy(j):
        src = o_loc.at[z, j, 0:heads, pl.ds(pl.multiple_of(other * rows, rows), rows), :]
        return remote(src, f_recv.at[j], fs_sem.at[j], fr_sem.at[j], z, other)

    for copy in hid_copy():
        copy.start()
    for k in range(CHUNKS):
        wo_copy(k).start()
    barrier = pltpu.get_barrier_semaphore()
    pl.semaphore_signal(barrier, inc=1, device_id={"seq": near, "sub": c}, device_id_type=MESH)
    pl.semaphore_signal(barrier, inc=1, device_id={"seq": z, "sub": other}, device_id_type=MESH)

    @pl.when(inner)
    def _():
        pl.semaphore_signal(
            barrier, inc=1, device_id={"seq": far_in, "sub": c}, device_id_type=MESH
        )

    words = [
        jnp.where(z < 2, jnp.where(z == 0, w[0], w[1]), jnp.where(z == 2, w[2], w[3]))
        for w in zip(*(packed_plan(steps) for steps in PLAN))
    ]

    def step_at(n):
        at = lax.div(n, 3)
        level = words
        bit = 1
        while len(level) > 1:
            odd = lax.rem(lax.div(at, bit), 2) == 1
            level = [
                jnp.where(odd, level[i + 1], level[i]) if i + 1 < len(level) else level[i]
                for i in range(0, len(level), 2)
            ]
            bit *= 2
        word = level[0]
        which = lax.rem(n, 3)
        word = jnp.where(
            which == 0, word, jnp.where(which == 1, lax.div(word, 1024), lax.div(word, 1048576))
        )
        return lax.rem(word, 1024)

    kn[...] = jnp.zeros_like(kn)
    vn[...] = jnp.zeros_like(vn)

    pl.semaphore_wait(barrier, jnp.where(inner, 3, 2))

    for copy in hid_copy():
        copy.wait()

    def pair_sum(k):
        pair_copy(k).wait_recv()
        both = own_part[k] + p_recv[k].astype(F32)
        part[k] = both.astype(BF).reshape(Z, rows, cw)

        @pl.when(outer)
        def _():
            out_copy(k, ORDER[0]).start()

    def stage_a(k, carry):
        wo_copy(k).wait()
        lhs = hid_v[...].reshape(span, hid.shape[3])
        half = Z * rows

        def go(t, carry):
            cols = pl.ds(pl.multiple_of(t * TILE, TILE), TILE)
            value = jnp.dot(lhs, wo_v[k, :, cols], preferred_element_type=F32)
            p_send[k, :, cols] = value[:half].astype(BF)
            own_part[k, :, cols] = value[half:]
            return carry

        lax.fori_loop(0, cw // TILE, go, 0)
        pair_copy(k).start()

        @pl.when(k >= 1)
        def _():
            pair_sum(k - 1)

        return carry

    lax.fori_loop(0, CHUNKS, stage_a, 0)
    for copy in w_copies():
        copy.start()
    pair_sum(CHUNKS - 1)

    @pl.when(outer)
    def _():
        for r in ORDER[1:]:
            for k in range(CHUNKS):
                out_copy(k, r).start()

    for i in range(2):
        for j in range(Z):
            kv_local(i, j).start()
            kv_remote(i, j).start()

    angle = (starts[0] + lax.broadcasted_iota(jnp.int32, (span, HD), 0)).astype(F32) * freqs[...]
    rope_v[0] = jnp.cos(angle)
    sines = jnp.sin(angle)
    first = lax.broadcasted_iota(jnp.int32, (span, HD), 1) < HD // 2
    rope_v[1] = jnp.where(first, -sines, sines)

    length = lengths[0]
    slots = z * 2 * wl + lax.broadcasted_iota(jnp.int32, (1, 2 * wl), 1)
    live = slots < length
    c2 = math.log2(math.e) / math.sqrt(HD)
    nt = (((1,), (1,)), ((), ()))
    lane = lax.broadcasted_iota(jnp.int32, (pair, HD), 1)

    def add_near(k, r):
        out_copy(k, r).wait_recv()
        both = part[k, r].astype(F32) + part_in[k, r].astype(F32)
        side[k, r] = both.astype(BF)
        mid_copy(k, r).start()

    def add_far(k, r):
        @pl.when(inner)
        def _():
            mid_copy(k, r).wait_recv()
            both = side[k, r].astype(F32) + side_in[k, r].astype(F32)
            x_all[k, 2 * r + c] = both.astype(BF)
            x_copy(k, r).start()

        @pl.when(outer)
        def _():
            x_copy(k, r).wait_recv()

        fw_copy(k, r, c).start()

    def project(r):
        squares = jnp.zeros((pair, 1), F32)
        for k in range(CHUNKS):
            fw_copy(k, r, other).wait_recv()
            x = x_all[k, pl.ds(2 * r, 2)].reshape(pair, cw).astype(F32)
            squares = squares + jnp.sum(x * x, axis=-1, keepdims=True)
            cols = slice(k * cw, (k + 1) * cw)
            xg_v[:, cols] = (x * gain[cols].astype(F32).reshape(1, cw)).astype(BF)
        inverse = lax.rsqrt(squares * (1.0 / width) + EPS)
        acc = jnp.dot(xg_v[...], w_v[...], preferred_element_type=F32)
        at = pl.ds(pl.multiple_of(r * pair, pair), pair)
        cosine = rope_v[0, at, :]
        sine = rope_v[1, at, :]

        def rope(value):
            return value * cosine + pltpu.roll(value, HD // 2, 1) * sine

        for h in range(heads):
            value = acc[:, h * HD : (h + 1) * HD] * inverse
            q_all[r, z, h] = (rope(value) * c2).astype(BF)
        q_copy(r, z, 0, near).start()

        @pl.when(inner)
        def _():
            q_copy(r, z, 1, far_in).start()

        key_raw = (acc[:, ql : ql + HD] * inverse).astype(BF)
        kn[at, :] = rope(key_raw.astype(F32)).astype(BF)
        vn[at, :] = (acc[:, ql + HD : ql + 2 * HD] * inverse).astype(BF)

    def stats_of(lse):
        stats = jnp.zeros((pair, HD), F32)
        for h in range(heads):
            stats = jnp.where(
                (lane == h) | (lane == h + heads), lse[h * pair : (h + 1) * pair], stats
            )
        return stats

    def packed(stats):
        high = stats.astype(BF).astype(F32)
        return jnp.where(lane < heads, high, stats - high).astype(BF)

    def unpacked(block):
        both = block.astype(F32)
        return both + pltpu.roll(both, HD - heads, 1)

    def blend(r, j, part_of, stats):
        mine = unpacked(o_loc[r, j, heads])
        best = jnp.maximum(mine, stats)
        a = jnp.exp2(mine - best)
        b = jnp.exp2(stats - best)
        total = a + b
        inv = 1.0 / total
        a = a * inv
        b = b * inv
        for h in range(heads):
            mix = a[:, h : h + 1] * o_loc[r, j, h].astype(F32) + b[:, h : h + 1] * part_of(h)
            o_loc[r, j, h] = mix.astype(BF)
        lse = best + jnp.log2(total)
        lse = jnp.where(lane < heads, lse, pltpu.roll(lse, heads, 1))
        o_loc[r, j, heads] = packed(lse)

    def softmaxed(s, values):
        top = jnp.max(s, axis=-1, keepdims=True)
        p = jnp.exp2(s - top)
        total = jnp.sum(p, axis=-1, keepdims=True)
        mixed = jnp.dot(p.astype(BF), values, preferred_element_type=F32)
        return mixed * (1.0 / total), top + jnp.log2(total)

    def attend(r, j):
        @pl.when(outer & (j != z))
        def _():
            q_copy(r, j, 0, near).wait_recv()

        q = q_all[r, j].reshape(stack, HD)
        s = lax.dot_general(q, k_v[j], nt, preferred_element_type=F32)
        s = jnp.where(live, s, NEG)
        mixed, lse = softmaxed(s, v_v[j])
        o_loc[r, j, 0:heads] = mixed.astype(BF).reshape(heads, pair, HD)
        o_loc[r, j, heads] = packed(stats_of(lse))

        @pl.when(j == z)
        def _():
            s2 = lax.dot_general(q_all[r, j].reshape(stack, HD), kn[...], nt, preferred_element_type=F32)
            at = lax.rem(lax.broadcasted_iota(jnp.int32, (stack, span), 0), pair) + r * pair
            t = lax.broadcasted_iota(jnp.int32, (stack, span), 1)
            s2 = jnp.where(t <= at, s2, NEG)
            mixed, lse = softmaxed(s2, vn[...])
            blend(r, j, lambda h: mixed[h * pair : (h + 1) * pair], stats_of(lse))

        @pl.when(outer & (z != r))
        def _():
            o_copy(r, j).start()

    def merge(r, j):
        def one(way, carry):
            has = jnp.where(way == 0, (z >= 1) & (z <= r), (z <= Z - 2) & (z >= r))

            @pl.when(has)
            def _():
                remote(
                    o_loc.at[r, j], o_in.at[r, j, way], os_sem.at[r, j], or_sem.at[r, j, way], near, c
                ).wait_recv()
                blend(
                    r, j, lambda h: o_in[r, j, way, h].astype(F32), unpacked(o_in[r, j, way, heads])
                )

            return carry

        lax.fori_loop(0, 2, one, 0)

        @pl.when(z != r)
        def _():
            o_copy(r, j).start()

        @pl.when(z == r)
        def _():
            f_copy(j).start()
            keep = pl.ds(pl.multiple_of(c * rows, rows), rows)
            for h in range(heads):
                col = pl.ds(pl.multiple_of((2 * j + c) * ql + h * HD, HD), HD)
                out[0, :, col] = o_loc[r, j, h, keep, :]

    def pass_on(r, j):
        q_copy(r, j, 0, near).wait_recv()

        @pl.when(j == near)
        def _():
            q_copy(r, j, 2, far_in).start()

        @pl.when(j != near)
        def _():
            q_copy(r, j, jnp.where(j == far_in, 3, 4), near).start()

    def need_w():
        for copy in w_copies():
            copy.wait()

    def need_kv():
        for i in range(2):
            for j in range(Z):
                kv_local(i, j).wait()
                kv_remote(i, j).wait_recv()

    def run(n, carry):
        step = step_at(n)
        kind = lax.div(step, 64)
        a = lax.rem(lax.div(step, 8), 8)
        b = lax.rem(step, 8)
        for code, what in (
            (LEFT, lambda: add_near(a, b)),
            (FULL, lambda: add_far(a, b)),
            (QKV, lambda: project(a)),
            (ATTEND, lambda: attend(a, b)),
            (MERGE, lambda: merge(a, b)),
            (PASS, lambda: pass_on(a, b)),
            (NEED_W, need_w),
            (NEED_KV, need_kv),
        ):
            pl.when(kind == code)(what)
        return carry

    lax.fori_loop(0, len(PLAN[0]), run, 0)

    for j in range(Z):
        f_copy(j).wait_recv()
        for h in range(heads):
            col = pl.ds(pl.multiple_of((2 * j + other) * ql + h * HD, HD), HD)
            out[0, :, col] = f_recv[j, h]

    for j in range(Z):
        f_copy(j).wait_send()
    for i in range(2):
        for j in range(Z):
            kv_remote(i, j).wait_send()

    def drain(k, carry):
        pair_copy(k).wait_send()
        for r in range(Z):
            fw_copy(k, r, c).wait_send()

            @pl.when(outer)
            def _():
                out_copy(k, r).wait_send()

            @pl.when(inner)
            def _():
                mid_copy(k, r).wait_send()
                x_copy(k, r).wait_send()

        return carry

    lax.fori_loop(0, CHUNKS, drain, 0)

    def drain_q(r, carry):
        q_copy(r, z, 0, near).wait_send()

        @pl.when(inner)
        def _():
            for sem in range(1, 5):
                q_copy(r, z, sem, near).wait_send()

        @pl.when(z != r)
        def _():
            for j in range(Z):
                o_copy(r, j).wait_send()

        return carry

    lax.fori_loop(0, Z, drain_q, 0)


def fused(gen_hidden, out_proj, norm_gain, q_weight, kv_weight, kv_cache, lengths, span_start):
    Z = lax.axis_size("seq")
    _, span, dl = gen_hidden.shape
    rows = span // (2 * Z)
    width = out_proj.shape[1]
    cw = width // CHUNKS
    ql = q_weight.shape[1]
    heads = ql // HD
    wl = kv_cache.shape[2]
    half = HD // 2
    freq = THETA ** (-np.arange(half, dtype=np.float64) * 2.0 / HD)
    freqs = jnp.asarray(np.concatenate([freq, freq])[None, :].astype(np.float32))
    any_spec = pl.BlockSpec(memory_space=pl.ANY)
    vm_spec = pl.BlockSpec(memory_space=pltpu.VMEM)
    sm_spec = pl.BlockSpec(memory_space=pltpu.SMEM)
    dma = pltpu.SemaphoreType.DMA
    V = pltpu.VMEM
    return pl.pallas_call(
        functools.partial(fused_kernel, Z),
        out_shape=jax.ShapeDtypeStruct((1, rows, 2 * Z * ql), BF),
        in_specs=[any_spec, any_spec, vm_spec, any_spec, any_spec, any_spec, sm_spec, sm_spec, vm_spec],
        out_specs=vm_spec,
        scratch_shapes=[
            V((2, Z, rows, dl), BF),
            V((CHUNKS, dl, cw), BF),
            V((width, ql + 2 * HD), BF),
            V((Z, 2 * wl, HD), BF),
            V((Z, 2 * wl, HD), BF),
            V((CHUNKS, Z * rows, cw), BF),
            V((CHUNKS, Z * rows, cw), BF),
            V((CHUNKS, Z * rows, cw), F32),
            V((CHUNKS, Z, rows, cw), BF),
            V((CHUNKS, Z, rows, cw), BF),
            V((CHUNKS, Z, rows, cw), BF),
            V((CHUNKS, Z, rows, cw), BF),
            V((CHUNKS, 2 * Z, rows, cw), BF),
            V((2 * rows, width), BF),
            V((Z, Z, heads, 2 * rows, HD), BF),
            V((span, HD), BF),
            V((span, HD), BF),
            V((Z, Z, heads + 1, 2 * rows, HD), BF),
            V((Z, Z, 2, heads + 1, 2 * rows, HD), BF),
            V((Z, heads, rows, HD), BF),
            V((2, span, HD), F32),
            dma((5,)),
            dma((CHUNKS,)),
            dma((2, Z)),
            dma((2, Z)),
            dma((2, Z)),
            dma((CHUNKS,)),
            dma((CHUNKS,)),
            dma((CHUNKS, Z)),
            dma((CHUNKS, Z)),
            dma((CHUNKS, Z)),
            dma((CHUNKS, Z)),
            dma((CHUNKS, Z)),
            dma((CHUNKS, Z)),
            dma((CHUNKS, Z)),
            dma((CHUNKS, Z)),
            dma((Z, 5)),
            dma((Z, Z)),
            dma((Z, Z)),
            dma((Z, Z, 2)),
            dma((Z,)),
            dma((Z,)),
        ],
        compiler_params=pltpu.CompilerParams(
            collective_id=0, has_side_effects=True, vmem_limit_bytes=64000000
        ),
    )(
        gen_hidden.reshape(Z, 2, rows, dl),
        out_proj,
        norm_gain,
        q_weight,
        kv_weight,
        kv_cache.reshape(2, wl, KVH * HD),
        lengths,
        span_start,
        freqs,
    )


def solution(mesh):
    placed = (
        P(("groups", "batch"), None, ("seq", "sub")),
        P(("seq", "sub"), None),
        P(),
        P(None, ("seq", "sub")),
        P(None, None, ("seq", "sub")),
        P(None, ("groups", "batch"), ("seq", "sub"), None),
        P(("groups", "batch")),
        P(("groups", "batch")),
    )
    aligned = mesh.shape["sub"] == 2 and mesh.shape["seq"] * 2 == KVH
    return jax.shard_map(
        fused if aligned else body,
        mesh=mesh,
        in_specs=placed,
        out_specs=P(("groups", "batch"), ("seq", "sub"), None),
        check_vma=False,
    )
```

time: 104 us -> 81.4 us (0.78); the launches traced: 102 us -> 81.2 us
  Pallas kernels: 98.7 us -> 78.2 us
    pallas_call x1, Pallas kernels: 98.7 us -> 78.2 us  [fused(): pl.pallas_call(functools.partial(fused_kernel, Z), out_shape=jax.ShapeDty...]
where the time goes in v1:
time: 81.4 us; the launch traced here: 81.2 us
  Pallas kernels  78.2 us (96%)
  local copies, waits for them, and re-layouts  1.67 us (2%)
  between operations  1.3 us (2%)
    pallas_call x1, Pallas kernels, fused(): pl.pallas_call(functools.partial(fused_kernel, Z), out_shape=jax.ShapeDty...  78.2 us
    unnamed x1, local copies, waits for them, and re-layouts  1.67 us

profile of v1, /device:TPU:28, one launch (start us, length us, event | category | flops | bytes accessed | tf_op | source)
XLA Modules:
  0.0 81.2 jit_solution(10026920510612901410)
XLA Ops:
  1.3 78.2 %shard_map.91 = bf16[1,32,4096]{2,1,0:T(8,128)(2,1)} custom-call(bf16[4,2,32,1024]{3,2,1,0:T(8,128)(2,1)} %bitcast.3, bf16[1024,4096]{1,0:T(8,128)(2,1)} %wo.1, bf16[4096]{0:T(1024)(128)(2,1)} %gain.1, bf16[4096,512]{1,0:T(8,128)(2,1)} %wq.1, bf16[2,4096,128]{2,1,0:T(8,128)(2,1)} %wkv.1, bf16[2,1024,1024]{2,1,0:T(8,128)(2,1)} %bitcast.2, ...), custom_call_target="tpu_custom_call" | custom-call | tf_op jit(solution)/shard_map/pallas_call | solution.py:676
  79.5 1.7 %copy.13 = bf16[1,32,4096]{2,1,0:T(8,128)(2,1)} copy(bf16[1,32,4096]{2,1,0:T(8,128)(2,1)} %shard_map.91) | data formatting | bytes 524288
